TPU v7x, 32 devices: a whole 2x2x4 slice. The times are simulated.
32 devices in a mesh: dp: 8 (over z, core), tensor: 4 (over y, x).
Axes of the slice: x: 2, y: 2, z: 4, core: 2. Of those that a mesh axis runs over, the one named last changes fastest.
Arguments:
- hidden_acts: bfloat16 [16384, 14336], P('dp', 'tensor'), may hold values from -6 to 6
- out_grads: bfloat16 [16384, 4096], P('dp', 'tensor'), may hold values from -6 to 6
- proj_in: bfloat16 [14336, 64], P('tensor'), may hold values from -0.046875 to 0.046875
- proj_out: bfloat16 [4096, 64], P('tensor'), may hold values from -0.09375 to 0.09375
- segments: int32 [32, 16384], P(None, 'dp'), may hold values from 0 to 1, as said below
- doc_counts: int32 [8], P('dp'), may hold values from 10 to 32
Outputs:
- doc_grads: bfloat16 [256, 4096], P('dp', 'tensor')
- fisher: float32 [4096, 4096], P('dp', 'tensor')
Inputs may be any that keep to these rules, and one draw needn't show every extreme that they name: `segments`: every token belongs to exactly one slot of its shard; within one shard's 2048 tokens the slots 0 to 31 are contiguous runs in that order, each holding at least one token.
All inputs are finite; a program needn't handle non-finite values.
Results may differ from a plain program's by a relative error of at most 0.0062.
Values may be sent and summed in bfloat16 or wider, within the bound.
No kernel may reach another device: no remote copies, remote signals or barrier semaphores. Data moves between devices by JAX's collectives and lax.ppermute only.
A program may use at most 64 MiB of HBM per device.

v0:
```python
import jax
import jax.numpy as jnp
from jax import lax
from jax.sharding import PartitionSpec as P

RANK = 64


def doc_sums_of(seg_live, dy_proj, x_proj):
    row_count = x_proj.shape[0]
    block_rows = 512
    summed = jnp.zeros((seg_live.shape[0], RANK * RANK), jnp.float32)
    for offset in range(0, row_count, block_rows):
        outer = (
            (
                dy_proj[offset : offset + block_rows, :, None]
                * x_proj[offset : offset + block_rows, None, :]
            )
            .reshape(block_rows, RANK * RANK)
            .astype(jnp.bfloat16)
        )
        summed = summed + jnp.dot(
            seg_live[:, offset : offset + block_rows], outer, preferred_element_type=jnp.float32
        )
    return summed


def transpose_product(left, right):
    return lax.dot_general(
        left, right, (((0,), (0,)), ((), ())), preferred_element_type=jnp.float32
    )


def per_device(hidden_acts, out_grads, proj_in, proj_out, segments, doc_counts):
    x_part = jnp.dot(hidden_acts, proj_in, preferred_element_type=jnp.float32)
    dy_part = jnp.dot(out_grads, proj_out, preferred_element_type=jnp.float32)
    partial_proj = jnp.concatenate([dy_part, x_part], axis=1)
    doc_total = segments.shape[0]
    live_docs = (jnp.arange(doc_total, dtype=jnp.int32) < doc_counts[0]).astype(jnp.int32)
    seg_int = segments * live_docs[:, None]
    seg_live = seg_int.astype(jnp.bfloat16)
    local_tokens = jnp.sum(seg_int).astype(jnp.float32)
    stacked = lax.psum(partial_proj, "tensor")
    doc_sums = doc_sums_of(seg_live, stacked[:, :RANK], stacked[:, RANK:])
    doc_grads = doc_sums.astype(jnp.bfloat16)
    col_width = doc_grads.shape[1] // lax.axis_size("tensor")
    col_block = lax.dynamic_slice_in_dim(
        doc_grads, lax.axis_index("tensor") * col_width, col_width, 1
    )
    total_tokens = lax.psum(local_tokens, "dp")
    dp_size = lax.axis_size("dp")
    row_width = doc_grads.shape[1] // dp_size
    split_rows = doc_grads.reshape(doc_total, dp_size, row_width)
    gathered_rows = lax.all_to_all(
        split_rows, "dp", split_axis=1, concat_axis=0, tiled=True
    ).reshape(doc_total * dp_size, row_width)
    fisher_block = transpose_product(
        gathered_rows, lax.all_gather(col_block, "dp", axis=0, tiled=True)
    )
    return (col_block, fisher_block / total_tokens)


def solution(mesh):
    return jax.shard_map(
        per_device,
        mesh=mesh,
        in_specs=(
            P("dp", "tensor"),
            P("dp", "tensor"),
            P("tensor", None),
            P("tensor", None),
            P(None, "dp"),
            P("dp"),
        ),
        out_specs=(P("dp", "tensor"), P("dp", "tensor")),
        check_vma=False,
    )
```

profile of v0, /device:TPU:0, one launch (start us, length us, event | category | flops | bytes accessed | tf_op | source)
XLA Modules:
  0.0 138.1 jit_solution(17943158903537048808)
XLA Ops:
  7.2 0.0 copy-start
  7.2 0.0 all-reduce.2.cloned.1.call-start
  7.2 3.6 %fusion.7 = f32[2048,64]{0,1:T(8,128)S(1)} fusion(bf16[2048,1024]{1,0:T(8,128)(2,1)} %param.7, bf16[1024,64]{0,1:T(8,128)(2,1)} %param.9), kind=kOutput, calls=%fused_computation.21 | convolution fusion | flops 268435456 | bytes 4849664 | tf_op jit(solution)/shard_map/dot_general | solution.py:36
  10.9 0.0 copy-done
  10.9 0.0 copy-start.2
  10.9 9.7 %fusion.8 = f32[2048,64]{0,1:T(8,128)S(1)} fusion(bf16[2048,3584]{1,0:T(8,128)(2,1)} %param.6, bf16[3584,64]{0,1:T(8,128)(2,1)S(1)} %copy-done), kind=kOutput, calls=%fused_computation.22 | convolution fusion | flops 939524096 | bytes 15663104 | tf_op jit(solution)/shard_map/dot_general | solution.py:35
  20.6 1.0 pad_maximum_fusion
  21.6 0.0 all-reduce.2.cloned.1.call-update
  22.3 0.0 copy-done.2
  22.3 0.8 multiply_reduce_fusion
  23.1 53.9 %all-reduce.2.cloned.1.call-done = f32[2048,128]{0,1:T(8,128)} async-done(((f32[2048,128]{0,1:T(8,128)}), f32[2048,128]{0,1:T(8,128)}) %all-reduce.2.cloned.1.call-update) | async-done | bytes 1048592 | tf_op jit(solution)/shard_map/psum | solution.py:43
  77.0 1.4 fusion.6
  78.3 3.3 %multiply_convert_fusion.2 = (bf16[512,64,64]{0,2,1:T(8,128)(2,1)S(1)}, bf16[512,64,64]{0,2,1:T(8,128)(2,1)S(1)}) fusion(f32[512,64]{0,1:T(8,128)S(1)} %get-tuple-element.6, f32[512,64]{0,1:T(8,128)S(1)} %get-tuple-element.7, f32[512,64]{0,1:T(8,128)S(1)} %get-tuple-element.8, f32[512,64]{0,1:T(8,128)S(1)} %get-tuple-element.9), kind=kLoop, calls=%fused_computation.2 | loop fusion | flops 8388608 | bytes 8912896 | tf_op jit(solution)/shard_map/convert_element_type | solution.py:20
  81.6 1.3 fusion.4
  82.9 1.3 convolution_add_fusion.2
  84.2 3.3 %multiply_convert_fusion = (bf16[512,64,64]{0,2,1:T(8,128)(2,1)S(1)}, bf16[512,64,64]{0,2,1:T(8,128)(2,1)S(1)}) fusion(f32[512,64]{0,1:T(8,128)S(1)} %get-tuple-element.3, f32[512,64]{0,1:T(8,128)S(1)} %get-tuple-element.2, f32[512,64]{0,1:T(8,128)S(1)} %get-tuple-element.4, f32[512,64]{0,1:T(8,128)S(1)} %get-tuple-element.5), kind=kLoop, calls=%fused_computation | loop fusion | flops 8388608 | bytes 8912896 | tf_op jit(solution)/shard_map/convert_element_type | solution.py:20
  87.5 1.3 convolution_add_fusion.1
  88.8 1.3 fusion
  90.2 0.7 copy.19
  90.9 4.6 %all-to-all-start = ((bf16[32,8,512]{2,0,1:T(8,128)(2,1)}), bf16[32,8,512]{2,0,1:T(8,128)(2,1)S(1)}, u32[]{:S(2)}, u32[]{:S(2)}) async-start(bf16[32,8,512]{2,0,1:T(8,128)(2,1)} %bitcast.23), calls=%async_computation | async-start | bytes 524288 | tf_op jit(solution)/shard_map/all_to_all | solution.py:54
  96.2 17.8 %psum.15 = f32[]{:T(128)} all-reduce(f32[]{:T(128)S(6)} %convert_element_type.51), channel_id=1, replica_groups=mesh['dp'=8,'tensor'=4] {'dp'}, use_global_device_ids=true, to_apply=%region_2.0 | all-reduce | flops 1 | bytes 8 | tf_op jit(solution)/shard_map/psum | solution.py:50
  113.9 14.9 %all_gather.3 = bf16[256,1024]{1,0:T(8,128)(2,1)S(1)} all-gather(bf16[32,1024]{1,0:T(8,128)(2,1)S(1)} %constant_dynamic-slice_fusion), channel_id=1, replica_groups=mesh['dp'=8,'tensor'=4] {'dp'}, dimensions={0}, use_global_device_ids=true | all-gather | bytes 589824 | tf_op jit(solution)/shard_map/all_gather | solution.py:58
  128.9 0.0 all-to-all-done
  128.9 2.4 %convolution_divide_fusion = f32[512,1024]{1,0:T(8,128)} fusion(bf16[256,512]{1,0:T(8,128)(2,1)S(1)} %bitcast.30, bf16[256,1024]{1,0:T(8,128)(2,1)S(1)} %all_gather.3, f32[]{:T(128)} %psum.15), kind=kOutput, calls=%fused_computation.8 | convolution fusion | flops 268959744 | bytes 2883588 | tf_op jit(solution)/shard_map/dot_general | solution.py:29
  (4 shorter events, 0.0 us)
Async XLA Ops:
  7.2 3.7 %copy-start = (bf16[3584,64]{0,1:T(8,128)(2,1)S(1)}, bf16[3584,64]{0,1:T(8,128)(2,1)}, u32[]{:S(2)}) copy-start(bf16[3584,64]{0,1:T(8,128)(2,1)} %param.8) | copy-start | bytes 1376260
  7.2 69.8 %all-reduce.2.cloned.1.call-start = ((), (), s32[]{:S(2)}) async-start(), calls=%async_computation.1 | async-start | bytes 2097152 | tf_op jit(solution)/shard_map/psum | solution.py:43
  10.9 11.5 %copy-start.2 = (s32[32,2048]{1,0:T(8,128)S(1)}, s32[32,2048]{1,0:T(8,128)}, u32[]{:S(2)}) copy-start(s32[32,2048]{1,0:T(8,128)} %param.10) | copy-start | bytes 786436
  90.9 38.0 %all-to-all-start = ((bf16[32,8,512]{2,0,1:T(8,128)(2,1)}), bf16[32,8,512]{2,0,1:T(8,128)(2,1)S(1)}, u32[]{:S(2)}, u32[]{:S(2)}) async-start(bf16[32,8,512]{2,0,1:T(8,128)(2,1)} %bitcast.23), calls=%async_computation | async-start | bytes 524288 | tf_op jit(solution)/shard_map/all_to_all | solution.py:54
  113.9 17.3 %copy-start.1 = (bf16[32,1024]{1,0:T(8,128)(2,1)}, bf16[32,1024]{1,0:T(8,128)(2,1)S(1)}, u32[]{:S(2)}) copy-start(bf16[32,1024]{1,0:T(8,128)(2,1)S(1)} %constant_dynamic-slice_fusion) | copy-start | bytes 196612
Sparse Core Ops, SparseCore 0:
  21.8 55.1 all-reduce.1
where the time goes:
time: 138 us
  waiting for transfers between devices  53.9 us (39%)
  blocking collectives  32.7 us (24%)
  matrix products  21 us (15%)
  between operations  15.4 us (11%)
  other arithmetic  8.34 us (6%)
  starting transfers between devices  4.65 us (3%)
  local copies, waits for them, and re-layouts  2.11 us (2%)
    psum x1, waiting for transfers between devices, per_device(): stacked = lax.psum(partial_proj, 'tensor')  53.9 us
    psum x1, blocking collectives, per_device(): total_tokens = lax.psum(local_tokens, 'dp')  17.8 us
    all_gather x1, blocking collectives, per_device(): lax.all_gather(col_block, 'dp', axis=0, tiled=True)  14.9 us
    dot_general x1, matrix products, per_device(): x_part = jnp.dot(hidden_acts, proj_in, preferred_element_type=jnp.float32)  9.71 us
    convert_element_type x2, other arithmetic, doc_sums_of(): outer = (dy_proj[offset:offset + block_rows, :, None] * x_proj[offset:off...  6.53 us
    dot_general x4, matrix products, doc_sums_of(): jnp.dot(seg_live[:, offset:offset + block_rows], outer, preferred_element...  5.29 us
    all_to_all x1, starting transfers between devices, per_device(): lax.all_to_all(split_rows, 'dp', split_axis=1, concat_axis=0, tiled=True)  4.61 us
    dot_general x1, matrix products, per_device(): dy_part = jnp.dot(out_grads, proj_out, preferred_element_type=jnp.float32)  3.63 us
  transfers between devices with their start and end apart: 2, of which 1 were waited for; matrix products, arithmetic and copies ran while one was open for 1% of the time, Pallas kernels for 0%

commit v1 on v0

--- a/solution.py
+++ b/solution.py
@@ -40,7 +40,8 @@
     seg_int = segments * live_docs[:, None]
     seg_live = seg_int.astype(jnp.bfloat16)
     local_tokens = jnp.sum(seg_int).astype(jnp.float32)
-    stacked = lax.psum(partial_proj, "tensor")
+    top = lax.all_gather(partial_proj, "tensor")
+    stacked = jnp.sum(top, 0)
     doc_sums = doc_sums_of(seg_live, stacked[:, :RANK], stacked[:, RANK:])
     doc_grads = doc_sums.astype(jnp.bfloat16)
     col_width = doc_grads.shape[1] // lax.axis_size("tensor")

time: 138 us -> 148 us (1.072)
  other arithmetic: 8.34 us -> 13.2 us
  local copies, waits for them, and re-layouts: 2.11 us -> 6.88 us
    all_gather x0 -> x1, waiting for transfers between devices: none -> 54 us  [per_device(): top = lax.all_gather(partial_proj, 'tensor')]
    psum x1 -> x0, waiting for transfers between devices: 53.9 us -> none  [per_device(): stacked = lax.psum(partial_proj, 'tensor')]
    all_gather x0 -> x1, local copies, waits for them, and re-layouts: none -> 6.04 us  [per_device(): top = lax.all_gather(partial_proj, 'tensor')]
    reduce_sum x0 -> x1, other arithmetic: none -> 4.84 us  [per_device(): stacked = jnp.sum(top, 0)]
where the time goes in v1:
time: 148 us
  waiting for transfers between devices  54 us (36%)
  blocking collectives  32.7 us (22%)
  matrix products  21 us (14%)
  between operations  15.4 us (10%)
  other arithmetic  13.2 us (9%)
  local copies, waits for them, and re-layouts  6.88 us (5%)
  starting transfers between devices  4.65 us (3%)
    all_gather x1, waiting for transfers between devices, per_device(): top = lax.all_gather(partial_proj, 'tensor')  54 us
    psum x1, blocking collectives, per_device(): total_tokens = lax.psum(local_tokens, 'dp')  17.8 us
    all_gather x1, blocking collectives, per_device(): lax.all_gather(col_block, 'dp', axis=0, tiled=True)  14.9 us
    dot_general x1, matrix products, per_device(): x_part = jnp.dot(hidden_acts, proj_in, preferred_element_type=jnp.float32)  9.71 us
    convert_element_type x2, other arithmetic, doc_sums_of(): outer = (dy_proj[offset:offset + block_rows, :, None] * x_proj[offset:off...  6.53 us
    all_gather x1, local copies, waits for them, and re-layouts, per_device(): top = lax.all_gather(partial_proj, 'tensor')  6.04 us
    dot_general x4, matrix products, doc_sums_of(): jnp.dot(seg_live[:, offset:offset + block_rows], outer, preferred_element...  5.29 us
    reduce_sum x1, other arithmetic, per_device(): stacked = jnp.sum(top, 0)  4.84 us
  transfers between devices with their start and end apart: 2, of which 1 were waited for; matrix products, arithmetic and copies ran while one was open for 1% of the time, Pallas kernels for 0%

profile of v1, /device:TPU:0, one launch (start us, length us, event | category | flops | bytes accessed | tf_op | source)
XLA Modules:
  0.0 147.9 jit_solution(15985096232101240502)
XLA Ops:
  7.2 0.0 copy-start
  7.2 0.0 all-gather.3.cloned.1.call-start
  7.2 3.6 %fusion.7 = f32[2048,64]{0,1:T(8,128)S(1)} fusion(bf16[2048,1024]{1,0:T(8,128)(2,1)} %param.7, bf16[1024,64]{0,1:T(8,128)(2,1)} %param.9), kind=kOutput, calls=%fused_computation.21 | convolution fusion | flops 268435456 | bytes 4849664 | tf_op jit(solution)/shard_map/dot_general | solution.py:36
  10.9 0.0 copy-start.2
  10.9 9.7 %fusion.8 = f32[2048,64]{0,1:T(8,128)S(1)} fusion(bf16[2048,3584]{1,0:T(8,128)(2,1)} %param.6, bf16[3584,64]{0,1:T(8,128)(2,1)S(1)} %copy-done), kind=kOutput, calls=%fused_computation.22 | convolution fusion | flops 939524096 | bytes 15663104 | tf_op jit(solution)/shard_map/dot_general | solution.py:35
  20.6 1.1 pad_maximum_fusion
  21.6 0.0 all-gather.3.cloned.1.call-update
  22.3 0.8 multiply_reduce_fusion
  23.1 54.0 %all-gather.3.cloned.1.call-done = f32[8192,128]{0,1:T(8,128)} async-done(((f32[2048,128]{0,1:T(8,128)}), f32[8192,128]{0,1:T(8,128)}) %all-gather.3.cloned.1.call-update) | async-done | bytes 4194320 | tf_op jit(solution)/shard_map/all_gather | solution.py:43
  77.1 6.0 %reshape.46 = f32[4,2048,128]{1,0,2:T(4,128)} reshape(f32[8192,128]{0,1:T(8,128)} %all-gather.3.cloned.1.call-done) | data formatting | bytes 8388608 | tf_op jit(solution)/shard_map/all_gather | solution.py:43
  83.2 4.8 %reduce_sum.18 = f32[2048,128]{0,1:T(8,128)S(1)} reduce(f32[4,2048,128]{1,0,2:T(4,128)} %reshape.46, f32[]{:T(128)} %constant.5.clone.1), dimensions={0}, to_apply=%region_0.0 | reduce | flops 786432 | bytes 5242884 | tf_op jit(solution)/shard_map/reduce_sum | solution.py:44
  88.0 0.1 fusion.6
  88.1 3.3 %multiply_convert_fusion.2 = (bf16[512,64,64]{0,2,1:T(8,128)(2,1)S(1)}, bf16[512,64,64]{0,2,1:T(8,128)(2,1)S(1)}) fusion(f32[512,64]{0,1:T(8,128)S(1)} %get-tuple-element.6, f32[512,64]{0,1:T(8,128)S(1)} %get-tuple-element.7, f32[512,64]{0,1:T(8,128)S(1)} %get-tuple-element.8, f32[512,64]{0,1:T(8,128)S(1)} %get-tuple-element.9), kind=kLoop, calls=%fused_computation.2 | loop fusion | flops 8388608 | bytes 8912896 | tf_op jit(solution)/shard_map/convert_element_type | solution.py:20
  91.4 1.3 fusion.4
  92.7 1.3 convolution_add_fusion.2
  94.0 3.3 %multiply_convert_fusion = (bf16[512,64,64]{0,2,1:T(8,128)(2,1)S(1)}, bf16[512,64,64]{0,2,1:T(8,128)(2,1)S(1)}) fusion(f32[512,64]{0,1:T(8,128)S(1)} %get-tuple-element.3, f32[512,64]{0,1:T(8,128)S(1)} %get-tuple-element.2, f32[512,64]{0,1:T(8,128)S(1)} %get-tuple-element.4, f32[512,64]{0,1:T(8,128)S(1)} %get-tuple-element.5), kind=kLoop, calls=%fused_computation | loop fusion | flops 8388608 | bytes 8912896 | tf_op jit(solution)/shard_map/convert_element_type | solution.py:20
  97.3 1.3 convolution_add_fusion.1
  98.6 1.3 fusion
  99.9 0.7 copy.11
  100.7 4.6 %all-to-all-start = ((bf16[32,8,512]{2,0,1:T(8,128)(2,1)}), bf16[32,8,512]{2,0,1:T(8,128)(2,1)S(1)}, u32[]{:S(2)}, u32[]{:S(2)}) async-start(bf16[32,8,512]{2,0,1:T(8,128)(2,1)} %bitcast.25), calls=%async_computation | async-start | bytes 524288 | tf_op jit(solution)/shard_map/all_to_all | solution.py:55
  105.9 17.8 %psum.7 = f32[]{:T(128)} all-reduce(f32[]{:T(128)S(6)} %convert_element_type.51), channel_id=1, replica_groups=mesh['dp'=8,'tensor'=4] {'dp'}, use_global_device_ids=true, to_apply=%region_2.0 | all-reduce | flops 1 | bytes 8 | tf_op jit(solution)/shard_map/psum | solution.py:51
  123.7 14.9 %all_gather.11 = bf16[256,1024]{1,0:T(8,128)(2,1)S(1)} all-gather(bf16[32,1024]{1,0:T(8,128)(2,1)S(1)} %constant_dynamic-slice_fusion), channel_id=1, replica_groups=mesh['dp'=8,'tensor'=4] {'dp'}, dimensions={0}, use_global_device_ids=true | all-gather | bytes 589824 | tf_op jit(solution)/shard_map/all_gather | solution.py:59
  138.6 0.0 all-to-all-done
  138.6 2.4 %convolution_divide_fusion = f32[512,1024]{1,0:T(8,128)} fusion(bf16[256,512]{1,0:T(8,128)(2,1)S(1)} %bitcast.32, bf16[256,1024]{1,0:T(8,128)(2,1)S(1)} %all_gather.11, f32[]{:T(128)} %psum.7), kind=kOutput, calls=%fused_computation.8 | convolution fusion | flops 268959744 | bytes 2883588 | tf_op jit(solution)/shard_map/dot_general | solution.py:29
  (6 shorter events, 0.0 us)
Async XLA Ops:
  7.2 3.7 %copy-start = (bf16[3584,64]{0,1:T(8,128)(2,1)S(1)}, bf16[3584,64]{0,1:T(8,128)(2,1)}, u32[]{:S(2)}) copy-start(bf16[3584,64]{0,1:T(8,128)(2,1)} %param.8) | copy-start | bytes 1376260
  7.2 69.9 %all-gather.3.cloned.1.call-start = ((), (), s32[]{:S(2)}) async-start(), calls=%async_computation.1 | async-start | bytes 5242880 | tf_op jit(solution)/shard_map/all_gather | solution.py:43
  10.9 11.5 %copy-start.2 = (s32[32,2048]{1,0:T(8,128)S(1)}, s32[32,2048]{1,0:T(8,128)}, u32[]{:S(2)}) copy-start(s32[32,2048]{1,0:T(8,128)} %param.10) | copy-start | bytes 786436
  100.7 38.0 %all-to-all-start = ((bf16[32,8,512]{2,0,1:T(8,128)(2,1)}), bf16[32,8,512]{2,0,1:T(8,128)(2,1)S(1)}, u32[]{:S(2)}, u32[]{:S(2)}) async-start(bf16[32,8,512]{2,0,1:T(8,128)(2,1)} %bitcast.25), calls=%async_computation | async-start | bytes 524288 | tf_op jit(solution)/shard_map/all_to_all | solution.py:55
  123.7 17.3 %copy-start.1 = (bf16[32,1024]{1,0:T(8,128)(2,1)}, bf16[32,1024]{1,0:T(8,128)(2,1)S(1)}, u32[]{:S(2)}) copy-start(bf16[32,1024]{1,0:T(8,128)(2,1)S(1)} %constant_dynamic-slice_fusion) | copy-start | bytes 196612
Sparse Core Ops, SparseCore 0:
  21.8 55.2 all-gather.2
